TPU v7x, 32 devices: a whole 2x2x4 slice. The times are simulated.
32 devices in a mesh: groups: 2 (over y), ctx: 8 (over z, x), col: 2 (over core).
Axes of the slice: x: 2, y: 2, z: 4, core: 2. Of those that a mesh axis runs over, the one named last changes fastest.
Arguments:
- activations: bfloat16 [2048, 4096], P(('groups', 'ctx'), 'col'), parts along dimension 0, may hold values from -6 to 6
- gradients: bfloat16 [2048, 14336], P(('groups', 'ctx'), 'col'), parts along dimension 0, may hold values from -6 to 6
- doc_ids: int32 [2048], P(('groups', 'ctx')), parts along dimension 0, may hold values from 0 to 11, as said below
- proj_in: bfloat16 [4096, 64], P('col'), may hold values from -0.046875 to 0.046875
- proj_out: bfloat16 [14336, 64], P('col'), may hold values from -0.0234375 to 0.0234375
- inverse: float32 [4096, 4096], P('col', 'ctx')
- store_rows: bfloat16 [2048, 4096], P(('groups', 'ctx', 'col')), parts along dimension 0, may hold values from -0.09375 to 0.09375
Outputs:
- scores: float32 [12, 2048], P(None, ('groups', 'ctx', 'col')), parts along dimension 1
There are 2 independent parts, one for each index of `groups`. A program takes and returns all parts, laid end to end along the dimension named above; an argument that names none is the same for every part. Nothing has to cross between parts.
Inputs may be any that keep to these rules, and one draw needn't show every extreme that they name: `doc_ids`: document numbers never fall and rise by at most one from a token to the next, starting at 0. Every aligned block of 128 tokens holds the last token of one or two documents; the last token of the sequence ends document 12 - 1.
All inputs are finite; a program needn't handle non-finite values.
Results may differ from a plain program's by a relative error of at most 0.0029.
Values may be sent and summed in bfloat16 or wider, within the bound.
A program may use at most 64 MiB of HBM per device.

v0:
```python
import jax
import jax.numpy as jnp
from jax import lax
from jax.sharding import PartitionSpec as P


def from_behind(block, axis, distance):
    devices = range(lax.axis_size(axis))
    route = [(i - distance, i) for i in devices if i - distance in devices]
    return lax.ppermute(block, axis, route)


def shards(activations, gradients, doc_ids, proj_in, proj_out, inverse, store_rows):
    left_part = jnp.dot(activations, proj_in, preferred_element_type=jnp.float32)
    right_part = jnp.dot(gradients, proj_out, preferred_element_type=jnp.float32)
    proj_left, proj_right = lax.psum((left_part, right_part), "col")
    proj_rank = proj_right.shape[1]
    half_rank = proj_rank // lax.axis_size("col")
    own_half = lax.dynamic_slice_in_dim(proj_left, lax.axis_index("col") * half_rank, half_rank, 1)
    first_doc = doc_ids[0]
    slot_index = doc_ids - first_doc
    onehot = (slot_index[:, None] == jnp.arange(3, dtype=jnp.int32)[None, :]).astype(jnp.float32)
    weighted = (onehot[:, :, None] * own_half[:, None, :]).reshape(own_half.shape[0], 3 * half_rank)
    local_sums = lax.dot_general(
        weighted,
        proj_right,
        (((0,), (0,)), ((), ())),
        precision=lax.Precision.HIGHEST,
        preferred_element_type=jnp.float32,
    ).reshape(3, half_rank * proj_rank)
    doc_count = 3 * lax.axis_size("ctx") // 2
    last_row = lax.dynamic_index_in_dim(local_sums, slot_index[-1], 0, keepdims=False)
    incoming, incoming_id = from_behind((last_row, doc_ids[-1].astype(jnp.float32)), "ctx", 1)
    matches = (incoming_id == first_doc.astype(jnp.float32)).astype(jnp.float32)
    head_row = local_sums[0] + matches * incoming
    owned_rows = jnp.stack([head_row, local_sums[1]])
    owned_ids = (first_doc + jnp.arange(2, dtype=jnp.int32)).astype(jnp.float32)
    gathered, gathered_ids = (
        lax.all_gather(owned_rows, "ctx", axis=0, tiled=True),
        lax.all_gather(owned_ids, "ctx", axis=0, tiled=True),
    )
    positions = jnp.arange(gathered.shape[0], dtype=jnp.int32)
    wanted = jnp.arange(doc_count, dtype=jnp.int32).astype(jnp.float32)
    found = gathered_ids[None, :] == wanted[:, None]
    chosen = jnp.max(jnp.where(found, positions[None, :], -1), axis=1)
    doc_grads = jnp.take(gathered, chosen, axis=0)
    partial_q = jnp.dot(
        doc_grads, inverse, precision=lax.Precision.HIGHEST, preferred_element_type=jnp.float32
    )
    precond = lax.psum(partial_q, "col").astype(jnp.bfloat16)
    return lax.dot_general(
        lax.all_gather(precond, "ctx", axis=1, tiled=True),
        store_rows,
        (((1,), (1,)), ((), ())),
        preferred_element_type=jnp.float32,
    )


def solution(mesh):
    in_specs = (
        P(("groups", "ctx"), "col"),
        P(("groups", "ctx"), "col"),
        P(("groups", "ctx")),
        P("col", None),
        P("col", None),
        P("col", "ctx"),
        P(("groups", "ctx", "col"), None),
    )
    out_specs = P(None, ("groups", "ctx", "col"))
    return jax.shard_map(shards, mesh=mesh, in_specs=in_specs, out_specs=out_specs, check_vma=False)
```

profile of v0, /device:TPU:0, one launch (start us, length us, event | category | flops | bytes accessed | tf_op | source)
XLA Modules:
  0.0 129.1 jit_solution(9993455877551389465)
XLA Ops:
  6.5 1.4 %fusion.8 = (s32[1]{0:T(128)}, s32[1]{0:T(128)}) fusion(s32[128]{0:T(128)} %param.9), kind=kLoop, calls=%fused_computation.23 | loop fusion | bytes 16 | tf_op jit(solution)/shard_map/slice | solution.py:33
  8.6 6.2 %collective-permute-start = (f32[]{:T(128)}, f32[]{:T(128)}, u32[]{:S(2)}, u32[]{:S(2)}) collective-permute-start(f32[]{:T(128)} %bitcast.3), channel_id=1, source_target_pairs={{0,2},{2,4},{4,6},{6,8},{8,10},{10,12},{12,14},{1,3},{3,5},{5,7},{... | collective-permute-start | bytes 20 | tf_op jit(solution)/shard_map/ppermute | solution.py:10
  14.7 2.0 %fusion.9 = f32[128,64]{0,1:T(8,128)} fusion(bf16[128,2048]{1,0:T(8,128)(2,1)} %param.7, bf16[2048,64]{0,1:T(8,128)(2,1)} %param.10), kind=kOutput, calls=%fused_computation.24 | convolution fusion | flops 33554432 | bytes 819200 | tf_op jit(solution)/shard_map/dot_general | solution.py:14
  16.7 2.5 %fusion.10 = f32[128,64]{0,1:T(8,128)} fusion(bf16[128,7168]{1,0:T(8,128)(2,1)S(1)} %copy-done, bf16[7168,64]{0,1:T(8,128)(2,1)} %param.11), kind=kOutput, calls=%fused_computation.25 | convolution fusion | flops 117440512 | bytes 2785280 | tf_op jit(solution)/shard_map/dot_general | solution.py:15
  19.3 1.3 broadcast_subtract_fusion
  20.6 1.2 dynamic-slice
  22.5 0.7 convert_dynamic-update-slice_fusion
  23.7 18.9 %all-reduce = f32[16]{0:T(128)S(1)} all-reduce(f32[16]{0:T(128)S(1)} %convert_dynamic-update-slice_fusion), channel_id=1, replica_groups=mesh['groups'=2,'ctx'=8,'col'=2] {'ctx'}, use_global_device_ids=true, to_apply=%add | all-reduce | flops 16 | bytes 128
  42.6 0.2 select_reduce_fusion
  42.8 0.6 slice.22
  46.0 0.7 constant_dynamic-slice_fusion.1
  46.8 1.0 fusion.11
  47.7 0.1 copy.16
  47.8 0.1 reshape.57
  48.0 2.5 %collective-permute-start.1 = (f32[2048]{0:T(1024)S(1)}, f32[2048]{0:T(1024)S(1)}, u32[]{:S(2)}, u32[]{:S(2)}) collective-permute-start(f32[2048]{0:T(1024)S(1)} %bitcast.24), channel_id=1, source_target_pairs={{0,2},{2,4},{4,6},{6,8},{8,10},{10,12},{12,14},{1,3},{3,5},{5,7},{... | collective-permute-start | bytes 24584 | tf_op jit(solution)/shard_map/ppermute | solution.py:10
  50.7 0.1 slice.24
  50.8 1.0 collective-permute-done.1
  51.8 30.7 %all-gather = f32[8,2,2048]{2,1,0:T(2,128)S(1)} all-gather(f32[1,2,2048]{2,1,0:T(2,128)S(1)} %maximum_bitcast_fusion), channel_id=1, replica_groups=mesh['groups'=2,'ctx'=8,'col'=2] {'ctx'}, dimensions={0}, use_global_device_ids=true | all-gather | bytes 147456 | tf_op jit(solution)/shard_map/all_gather | solution.py:39
  82.5 0.1 reshape.70
  82.6 0.6 gather_fusion
  83.2 4.3 %fusion = f32[12,512]{1,0:T(8,128)S(1)} fusion(f32[2048,512]{1,0:T(8,128)} %param.12, f32[12,2048]{1,0:T(8,128)S(1)} %gather_fusion, pred[12]{0:T(512)(128)(4,1)S(1)} %compare_and_fusion), kind=kOutput, calls=%fused_computation.1 | convolution fusion | flops 151019520 | bytes 4317196 | tf_op jit(solution)/shard_map/dot_general | solution.py:47
  87.5 3.4 %psum.23 = bf16[12,512]{1,0:T(8,128)(2,1)S(1)} all-reduce(f32[12,512]{1,0:T(8,128)S(1)} %fusion), channel_id=1, replica_groups=mesh['groups'=2,'ctx'=8,'col'=2] {'col'}, use_global_device_ids=true, to_apply=%region_3.4 | all-reduce | flops 6144 | bytes 36864 | tf_op jit(solution)/shard_map/psum | solution.py:50
  90.9 30.5 %all_gather.11 = bf16[12,4096]{1,0:T(8,128)(2,1)S(1)} all-gather(bf16[12,512]{1,0:T(8,128)(2,1)S(1)} %psum.23), channel_id=1, replica_groups=mesh['groups'=2,'ctx'=8,'col'=2] {'ctx'}, dimensions={1}, use_global_device_ids=true | all-gather | bytes 110592 | tf_op jit(solution)/shard_map/all_gather | solution.py:52
  121.4 0.9 fusion.12
  (22 shorter events, 0.4 us)
Async XLA Ops:
  6.5 10.2 %copy-start = (bf16[128,7168]{1,0:T(8,128)(2,1)S(1)}, bf16[128,7168]{1,0:T(8,128)(2,1)}, u32[]{:S(2)}) copy-start(bf16[128,7168]{1,0:T(8,128)(2,1)} %param.8) | copy-start | bytes 5505028
  6.5 39.5 %all-reduce.4.cloned.1.call-start = ((), (), s32[]{:S(2)}) async-start(), calls=%async_computation | async-start | bytes 131072 | tf_op jit(solution)/shard_map/psum | solution.py:16
  8.6 36.8 %collective-permute-start = (f32[]{:T(128)}, f32[]{:T(128)}, u32[]{:S(2)}, u32[]{:S(2)}) collective-permute-start(f32[]{:T(128)} %bitcast.3), channel_id=1, source_target_pairs={{0,2},{2,4},{4,6},{6,8},{8,10},{10,12},{12,14},{1,3},{3,5},{5,7},{... | collective-permute-start | bytes 20 | tf_op jit(solution)/shard_map/ppermute | solution.py:10
  19.3 102.1 %copy-start.1 = (bf16[64,4096]{1,0:T(8,128)(2,1)S(1)}, bf16[64,4096]{1,0:T(8,128)(2,1)}, u32[]{:S(2)}) copy-start(bf16[64,4096]{1,0:T(8,128)(2,1)} %param.13) | copy-start | bytes 1572868
  48.0 3.9 %collective-permute-start.1 = (f32[2048]{0:T(1024)S(1)}, f32[2048]{0:T(1024)S(1)}, u32[]{:S(2)}, u32[]{:S(2)}) collective-permute-start(f32[2048]{0:T(1024)S(1)} %bitcast.24), channel_id=1, source_target_pairs={{0,2},{2,4},{4,6},{6,8},{8,10},{10,12},{12,14},{1,3},{3,5},{5,7},{... | collective-permute-start | bytes 24584 | tf_op jit(solution)/shard_map/ppermute | solution.py:10
Sparse Core Ops, SparseCore 0:
  19.4 18.0 all-reduce.3
where the time goes:
time: 130 us; the launch traced here: 129 us
  blocking collectives  83.5 us (64%)
  between operations  18 us (14%)
  matrix products  10.7 us (8%)
  starting transfers between devices  8.66 us (7%)
  local copies, waits for them, and re-layouts  5.17 us (4%)
  other arithmetic  2.17 us (2%)
    all_gather x1, blocking collectives, shards(): lax.all_gather(owned_rows, 'ctx', axis=0, tiled=True)  30.7 us
    all_gather x1, blocking collectives, shards(): lax.all_gather(precond, 'ctx', axis=1, tiled=True)  30.5 us
    unnamed x1, blocking collectives  18.9 us
    ppermute x2, starting transfers between devices, from_behind(): return lax.ppermute(block, axis, route)  8.66 us
    dot_general x1, matrix products, shards(): jnp.dot(doc_grads, inverse, precision=lax.Precision.HIGHEST, preferred_el...  4.29 us
    psum x1, blocking collectives, shards(): precond = lax.psum(partial_q, 'col').astype(jnp.bfloat16)  3.4 us
  transfers between devices with their start and end apart: 3, of which 1 were waited for; matrix products, arithmetic and copies ran while one was open for 7% of the time, Pallas kernels for 0%

commit v1 on v0

--- a/solution.py
+++ b/solution.py
@@ -1,6 +1,10 @@
+import functools
+
 import jax
 import jax.numpy as jnp
 from jax import lax
+from jax.experimental import pallas as pl
+from jax.experimental.pallas import tpu as pltpu
 from jax.sharding import PartitionSpec as P
 
 
@@ -56,6 +60,238 @@
     )
 
 
+LANES = 128
+SLOTS = 3
+CHUNKS = 4
+MESH = pl.DeviceIdType.MESH
+NT = (((1,), (1,)), ((), ()))
+
+
+def halves(value):
+    high = value.astype(jnp.bfloat16).astype(jnp.float32)
+    return high, value - high
+
+
+def dot_nt(left, right):
+    return lax.dot_general(left, right, NT, preferred_element_type=jnp.float32)
+
+
+def score_kernel(
+    n, cols, docs,
+    act, grad, ids, pin, pout, inv, store, out,
+    act_v, grad_v, pin_v, pout_v, inv_v, store_v, inv_hi, inv_lo,
+    ids_all, part_l, part_r, from_l, from_r, full_l, sums, q_part, q_from, q_all,
+    load_sem, ids_send, ids_recv, pair_send, pair_recv, sums_send, sums_recv, q_send, q_recv,
+):
+    me = lax.axis_index("ctx")
+    core = lax.axis_index("col")
+    other = cols - 1 - core
+    rank = pin.shape[0]
+    half = rank // cols
+    pack = LANES // rank
+    groups = half // pack
+    piece = SLOTS * groups
+    width = q_part.shape[2]
+
+    loads = [
+        pltpu.make_async_copy(ids, ids_all.at[me], load_sem.at[0]),
+        pltpu.make_async_copy(act, act_v, load_sem.at[1]),
+        pltpu.make_async_copy(pin, pin_v, load_sem.at[2]),
+    ]
+    step = grad.shape[1] // CHUNKS
+    for i in range(CHUNKS):
+        span = pl.ds(i * step, step)
+        loads.append(pltpu.make_async_copy(pout.at[:, span], pout_v.at[:, span], load_sem.at[3 + 2 * i]))
+        loads.append(pltpu.make_async_copy(grad.at[:, span], grad_v.at[:, span], load_sem.at[4 + 2 * i]))
+    loads.append(pltpu.make_async_copy(inv, inv_v, load_sem.at[3 + 2 * CHUNKS]))
+    loads.append(pltpu.make_async_copy(store, store_v, load_sem.at[4 + 2 * CHUNKS]))
+    for load in loads:
+        load.start()
+
+    barrier = pltpu.get_barrier_semaphore()
+    peers = []
+    for r in range(n):
+        for d in range(cols):
+            if r or d:
+                peers.append({"ctx": lax.rem(me + r, n), "col": lax.rem(core + d, cols)})
+    for peer in peers:
+        pl.semaphore_signal(barrier, inc=1, device_id=peer, device_id_type=MESH)
+
+    loads[1].wait()
+    loads[2].wait()
+    part_l[...] = dot_nt(pin_v[...], act_v[...])
+    pl.semaphore_wait(barrier, len(peers))
+
+    def remote(src, dst, send, recv, peer):
+        copy = pltpu.make_async_remote_copy(
+            src_ref=src, dst_ref=dst, send_sem=send, recv_sem=recv, device_id=peer, device_id_type=MESH
+        )
+        copy.start()
+        return copy
+
+    partner = {"col": other}
+    copy_l = remote(part_l.at[pl.ds(other * half, half)], from_l, pair_send.at[0], pair_recv.at[0], partner)
+    ids_copies = [
+        remote(ids, ids_all.at[me], ids_send.at[r], ids_recv.at[r], {"ctx": lax.rem(me + r, n)})
+        for r in range(1, n)
+    ]
+
+    right = None
+    for i in range(CHUNKS):
+        span = pl.ds(i * step, step)
+        loads[3 + 2 * i].wait()
+        loads[4 + 2 * i].wait()
+        term = dot_nt(pout_v[:, span], grad_v[:, span])
+        right = term if right is None else right + term
+    part_r[...] = right
+    copy_r = remote(part_r, from_r, pair_send.at[1], pair_recv.at[1], partner)
+
+    loads[0].wait()
+    own_ids = ids_all[me]
+    first = own_ids[:, 0:1]
+    masks = [(own_ids == first + s).astype(jnp.float32) for s in range(SLOTS)]
+    copy_l.wait_recv()
+    full_l[...] = part_l[pl.ds(pl.multiple_of(core * half, half), half), :] + from_l[...]
+    highs, lows = [], []
+    for p in range(pack):
+        rows = full_l[pl.ds(p, groups, stride=pack), :]
+        high, low = halves(jnp.concatenate([rows * mask for mask in masks], axis=0))
+        highs.append(high)
+        lows.append(low)
+    weights = jnp.concatenate(highs + highs + lows, axis=1).astype(jnp.bfloat16)
+    copy_r.wait_recv()
+    high, low = halves(part_r[...] + from_r[...])
+    zero = jnp.zeros_like(high)
+
+    def diagonal(block, p):
+        return [block if q == p else zero for q in range(pack)]
+
+    spread = jnp.concatenate(
+        [
+            jnp.concatenate(diagonal(high, p) + diagonal(low, p) + diagonal(high, p), axis=1)
+            for p in range(pack)
+        ],
+        axis=0,
+    ).astype(jnp.bfloat16)
+    mine = pl.ds(pl.multiple_of(me * piece, 8), piece)
+    sums[mine, :] = dot_nt(weights, spread)
+    sums_copies = [
+        remote(sums.at[mine], sums.at[mine], sums_send.at[r], sums_recv.at[r], {"ctx": lax.rem(me + r, n)})
+        for r in sorted(range(1, n), key=lambda r: -min(r, n - r))
+    ]
+
+    loads[3 + 2 * CHUNKS].wait()
+    band = LANES
+
+    def split(i, carry):
+        rows = pl.ds(pl.multiple_of(i * band, band), band)
+        high, low = halves(inv_v[rows, :])
+        inv_hi[rows, :] = high.astype(jnp.bfloat16)
+        inv_lo[rows, :] = low.astype(jnp.bfloat16)
+        return carry
+
+    lax.fori_loop(0, inv_v.shape[0] // band, split, 0)
+
+    for copy in ids_copies:
+        copy.wait_recv()
+    doc_rows = q_part.shape[1]
+    column = lax.broadcasted_iota(jnp.int32, (1, SLOTS * n), 1)
+    doc_of = jnp.zeros((1, SLOTS * n), jnp.int32)
+    for b in range(n):
+        inside = (column >= b * SLOTS) & (column < (b + 1) * SLOTS)
+        doc_of = jnp.where(inside, ids_all[b][:, 0:1] + (column - b * SLOTS), doc_of)
+    pick = (lax.broadcasted_iota(jnp.int32, (doc_rows, SLOTS * n), 0) == doc_of).astype(jnp.float32)
+
+    for copy in sums_copies:
+        copy.wait_recv()
+    gathered = jnp.concatenate(
+        [sums[pl.ds(k, SLOTS * n, stride=groups), :] for k in range(groups)], axis=1
+    )
+    high, low = halves(gathered)
+    both = jnp.concatenate([high, low], axis=0).astype(jnp.bfloat16)
+    main = jnp.dot(both, inv_hi[...], preferred_element_type=jnp.float32)
+    rest = jnp.dot(high.astype(jnp.bfloat16), inv_lo[...], preferred_element_type=jnp.float32)
+    rows = main[: SLOTS * n] + main[SLOTS * n :] + rest
+    picked = jnp.dot(pick, rows, precision=lax.Precision.HIGHEST, preferred_element_type=jnp.float32)
+    for c in range(cols):
+        q_part[c] = picked[:, c * width : (c + 1) * width]
+    copy_q = remote(q_part.at[other], q_from, pair_send.at[2], pair_recv.at[2], partner)
+    copy_q.wait_recv()
+    slot = me * cols + core
+    q_all[slot] = (q_part[core] + q_from[...]).astype(jnp.bfloat16)
+    q_copies = [
+        remote(q_all.at[slot], q_all.at[slot], q_send.at[i], q_recv.at[i], peers[i])
+        for i in sorted(range(len(peers)), key=lambda i: -min((i + 1) // cols, n - (i + 1) // cols))
+    ]
+    loads[4 + 2 * CHUNKS].wait()
+    for copy in q_copies:
+        copy.wait_recv()
+    precond = jnp.concatenate([q_all[i] for i in range(n * cols)], axis=1)
+    out[...] = dot_nt(precond, store_v[...])[:docs]
+    for copy in [copy_l, copy_r, copy_q] + ids_copies + sums_copies + q_copies:
+        copy.wait_send()
+
+
+def fused(n, cols, activations, gradients, doc_ids, proj_in, proj_out, inverse, store_rows):
+    tokens = activations.shape[0]
+    rank = proj_in.shape[1]
+    half = rank // cols
+    docs = SLOTS * n // 2
+    doc_rows = -(-docs // 16) * 16
+    width = inverse.shape[1] // cols
+    piece = SLOTS * half * rank // LANES
+    anywhere = pl.BlockSpec(memory_space=pl.ANY)
+    dma = pltpu.SemaphoreType.DMA
+    return pl.pallas_call(
+        functools.partial(score_kernel, n, cols, docs),
+        name="scores",
+        out_shape=jax.ShapeDtypeStruct((docs, store_rows.shape[0]), jnp.float32),
+        in_specs=[anywhere] * 7,
+        out_specs=pl.BlockSpec(memory_space=pltpu.VMEM),
+        scratch_shapes=[
+            pltpu.VMEM(activations.shape, jnp.bfloat16),
+            pltpu.VMEM(gradients.shape, jnp.bfloat16),
+            pltpu.VMEM(proj_in.shape[::-1], jnp.bfloat16),
+            pltpu.VMEM(proj_out.shape[::-1], jnp.bfloat16),
+            pltpu.VMEM(inverse.shape, jnp.float32),
+            pltpu.VMEM(store_rows.shape, jnp.bfloat16),
+            pltpu.VMEM(inverse.shape, jnp.bfloat16),
+            pltpu.VMEM(inverse.shape, jnp.bfloat16),
+            pltpu.VMEM((n, 1, tokens), jnp.int32),
+            pltpu.VMEM((rank, tokens), jnp.float32),
+            pltpu.VMEM((rank, tokens), jnp.float32),
+            pltpu.VMEM((half, tokens), jnp.float32),
+            pltpu.VMEM((rank, tokens), jnp.float32),
+            pltpu.VMEM((half, tokens), jnp.float32),
+            pltpu.VMEM((n * piece, LANES), jnp.float32),
+            pltpu.VMEM((cols, doc_rows, width), jnp.float32),
+            pltpu.VMEM((doc_rows, width), jnp.float32),
+            pltpu.VMEM((n * cols, doc_rows, width), jnp.bfloat16),
+            dma((5 + 2 * CHUNKS,)),
+            dma((n,)), dma((n,)),
+            dma((3,)), dma((3,)),
+            dma((n,)), dma((n,)),
+            dma((n * cols,)), dma((n * cols,)),
+        ],
+        compiler_params=pltpu.CompilerParams(
+            collective_id=0, has_side_effects=True, vmem_limit_bytes=60 << 20
+        ),
+    )(activations, gradients, doc_ids[None, :], proj_in.T, proj_out.T, inverse, store_rows)
+
+
+def suits_kernel(n, cols, activations, gradients, proj_in, inverse):
+    rank = proj_in.shape[1]
+    return (
+        cols == 2
+        and activations.shape[0] == LANES
+        and LANES % rank == 0
+        and (rank // cols * rank) % (8 * LANES) == 0
+        and gradients.shape[1] % (CHUNKS * LANES) == 0
+        and inverse.shape[1] % (cols * LANES) == 0
+        and n <= 16
+    )
+
+
 def solution(mesh):
     in_specs = (
         P(("groups", "ctx"), "col"),
@@ -67,4 +303,12 @@
         P(("groups", "ctx", "col"), None),
     )
     out_specs = P(None, ("groups", "ctx", "col"))
-    return jax.shard_map(shards, mesh=mesh, in_specs=in_specs, out_specs=out_specs, check_vma=False)
+    n, cols = mesh.shape["ctx"], mesh.shape["col"]
+
+    def body(activations, gradients, doc_ids, proj_in, proj_out, inverse, store_rows):
+        args = (activations, gradients, doc_ids, proj_in, proj_out, inverse, store_rows)
+        if suits_kernel(n, cols, activations, gradients, proj_in, inverse):
+            return fused(n, cols, *args)
+        return shards(*args)
+
+    return jax.shard_map(body, mesh=mesh, in_specs=in_specs, out_specs=out_specs, check_vma=False)

time: 130 us -> 25.6 us (0.20)
  blocking collectives: 83.5 us -> 0 us
  Pallas kernels: 0 us -> 24.1 us
  between operations: 18 us -> 0.01 us
  matrix products: 10.7 us -> 0 us
  starting transfers between devices: 8.66 us -> 0 us
  local copies, waits for them, and re-layouts: 5.17 us -> 1.3 us
  other arithmetic: 2.17 us -> 0 us
    all_gather x2 -> x0, blocking collectives: 61.2 us -> none  [the longest x1 30.7 us: shards(): lax.all_gather(owned_rows, 'ctx', axis=0, tiled=True)]
    pallas_call x0 -> x1, Pallas kernels: none -> 24.1 us  [fused(): pl.pallas_call(functools.partial(score_kernel, n, cols, docs), name='scor...]
    unnamed x1 -> x0, blocking collectives: 18.9 us -> none
    dot_general x5 -> x0, matrix products: 10.7 us -> none  [the longest x1 4.29 us: shards(): jnp.dot(doc_grads, inverse, precision=lax.Precision.HIGHEST, preferred_el...]
    ppermute x2 -> x0, starting transfers between devices: 8.66 us -> none  [from_behind(): return lax.ppermute(block, axis, route)]
    psum x1 -> x0, blocking collectives: 3.4 us -> none  [shards(): precond = lax.psum(partial_q, 'col').astype(jnp.bfloat16)]
    slice x6 -> x0, local copies, waits for them, and re-layouts: 2.26 us -> none  [the longest x1 1.39 us: shards(): doc_ids[-1].astype(jnp.float32)]
  transfers between devices with their start and end apart: 3 -> 0, of which waited for: 1 -> 0; matrix products, arithmetic and copies ran while one was open for 7% -> 0% of each run, Pallas kernels for 0% -> 0%
where the time goes in v1:
time: 25.6 us; the launch traced here: 25.4 us
  Pallas kernels  24.1 us (94%)
  local copies, waits for them, and re-layouts  1.3 us (5%)
    pallas_call x1, Pallas kernels, fused(): pl.pallas_call(functools.partial(score_kernel, n, cols, docs), name='scor...  24.1 us
    unnamed x1, local copies, waits for them, and re-layouts  1.3 us

profile of v1, /device:TPU:0, one launch (start us, length us, event | category | flops | bytes accessed | tf_op | source)
XLA Modules:
  0.0 25.4 jit_solution(15459817300404584245)
XLA Ops:
  0.0 24.1 %scores.1 = f32[12,64]{1,0:T(8,128)} custom-call(bf16[128,2048]{1,0:T(8,128)(2,1)} %act.1, bf16[128,7168]{1,0:T(8,128)(2,1)} %grad.1, s32[1,128]{1,0:T(1,128)} %bitcast.5, bf16[64,2048]{1,0:T(8,128)(2,1)} %bitcast.4, bf16[64,7168]{1,0:T(8,128)(2,1)} %bitcast.3, f32[2048,512]{1,0:T(8,128)} %inv.1, bf16[64,4096]{1,0:T(8,128)(2,1)} %store.1), custom_call_target="tpu_custom_call" | custom-call | tf_op jit(solution)/shard_map/scores/pallas_call | solution.py:245
  24.1 1.3 %copy.9 = f32[12,64]{1,0:T(8,128)} copy(f32[12,64]{1,0:T(8,128)} %scores.1) | data formatting | bytes 6144

commit v2 on v1

--- a/solution.py
+++ b/solution.py
@@ -64,6 +64,17 @@
 SLOTS = 3
 CHUNKS = 4
 MESH = pl.DeviceIdType.MESH
+def sums_order(n):
+    order = []
+    for r in range(1, n // 2 + 1):
+        order += [n - r, r] if n - r != r else [r]
+    return order
+
+
+def q_order(n):
+    return sums_order(n) + [0]
+
+
 NT = (((1,), (1,)), ((), ()))
 
 
@@ -80,7 +91,7 @@
     n, cols, docs,
     act, grad, ids, pin, pout, inv, store, out,
     act_v, grad_v, pin_v, pout_v, inv_v, store_v, inv_hi, inv_lo,
-    ids_all, part_l, part_r, from_l, from_r, full_l, sums, q_part, q_from, q_all,
+    store_t, ids_all, part_l, part_r, from_l, from_r, full_l, sums, q_part, q_from, q_all,
     load_sem, ids_send, ids_recv, pair_send, pair_recv, sums_send, sums_recv, q_send, q_recv,
 ):
     me = lax.axis_index("ctx")
@@ -109,18 +120,18 @@
         load.start()
 
     barrier = pltpu.get_barrier_semaphore()
-    peers = []
-    for r in range(n):
+    ctx_peers = {r: {"ctx": jnp.bitwise_xor(me, r)} for r in sums_order(n)}
+    peers = {}
+    for r in q_order(n):
         for d in range(cols):
             if r or d:
-                peers.append({"ctx": lax.rem(me + r, n), "col": lax.rem(core + d, cols)})
-    for peer in peers:
+                peers[cols * r + d] = {"ctx": jnp.bitwise_xor(me, r), "col": jnp.bitwise_xor(core, d)}
+    for peer in peers.values():
         pl.semaphore_signal(barrier, inc=1, device_id=peer, device_id_type=MESH)
 
     loads[1].wait()
     loads[2].wait()
     part_l[...] = dot_nt(pin_v[...], act_v[...])
-    pl.semaphore_wait(barrier, len(peers))
 
     def remote(src, dst, send, recv, peer):
         copy = pltpu.make_async_remote_copy(
@@ -128,13 +139,6 @@
         )
         copy.start()
         return copy
-
-    partner = {"col": other}
-    copy_l = remote(part_l.at[pl.ds(other * half, half)], from_l, pair_send.at[0], pair_recv.at[0], partner)
-    ids_copies = [
-        remote(ids, ids_all.at[me], ids_send.at[r], ids_recv.at[r], {"ctx": lax.rem(me + r, n)})
-        for r in range(1, n)
-    ]
 
     right = None
     for i in range(CHUNKS):
@@ -144,7 +148,14 @@
         term = dot_nt(pout_v[:, span], grad_v[:, span])
         right = term if right is None else right + term
     part_r[...] = right
+    pl.semaphore_wait(barrier, len(peers))
+    partner = {"col": other}
+    copy_l = remote(part_l.at[pl.ds(other * half, half)], from_l, pair_send.at[0], pair_recv.at[0], partner)
     copy_r = remote(part_r, from_r, pair_send.at[1], pair_recv.at[1], partner)
+    ids_copies = [
+        remote(ids, ids_all.at[me], ids_send.at[r], ids_recv.at[r], ctx_peers[r])
+        for r in ctx_peers
+    ]
 
     loads[0].wait()
     own_ids = ids_all[me]
@@ -176,8 +187,8 @@
     mine = pl.ds(pl.multiple_of(me * piece, 8), piece)
     sums[mine, :] = dot_nt(weights, spread)
     sums_copies = [
-        remote(sums.at[mine], sums.at[mine], sums_send.at[r], sums_recv.at[r], {"ctx": lax.rem(me + r, n)})
-        for r in sorted(range(1, n), key=lambda r: -min(r, n - r))
+        remote(sums.at[mine], sums.at[mine], sums_send.at[r], sums_recv.at[r], ctx_peers[r])
+        for r in ctx_peers
     ]
 
     loads[3 + 2 * CHUNKS].wait()
@@ -191,6 +202,8 @@
         return carry
 
     lax.fori_loop(0, inv_v.shape[0] // band, split, 0)
+    loads[4 + 2 * CHUNKS].wait()
+    store_t[...] = store_v[...].T
 
     for copy in ids_copies:
         copy.wait_recv()
@@ -221,13 +234,12 @@
     q_all[slot] = (q_part[core] + q_from[...]).astype(jnp.bfloat16)
     q_copies = [
         remote(q_all.at[slot], q_all.at[slot], q_send.at[i], q_recv.at[i], peers[i])
-        for i in sorted(range(len(peers)), key=lambda i: -min((i + 1) // cols, n - (i + 1) // cols))
+        for i in peers
     ]
-    loads[4 + 2 * CHUNKS].wait()
     for copy in q_copies:
         copy.wait_recv()
     precond = jnp.concatenate([q_all[i] for i in range(n * cols)], axis=1)
-    out[...] = dot_nt(precond, store_v[...])[:docs]
+    out[...] = jnp.dot(precond, store_t[...], preferred_element_type=jnp.float32)[:docs]
     for copy in [copy_l, copy_r, copy_q] + ids_copies + sums_copies + q_copies:
         copy.wait_send()
 
@@ -257,6 +269,7 @@
             pltpu.VMEM(store_rows.shape, jnp.bfloat16),
             pltpu.VMEM(inverse.shape, jnp.bfloat16),
             pltpu.VMEM(inverse.shape, jnp.bfloat16),
+            pltpu.VMEM(store_rows.shape[::-1], jnp.bfloat16),
             pltpu.VMEM((n, 1, tokens), jnp.int32),
             pltpu.VMEM((rank, tokens), jnp.float32),
             pltpu.VMEM((rank, tokens), jnp.float32),
@@ -289,6 +302,7 @@
         and gradients.shape[1] % (CHUNKS * LANES) == 0
         and inverse.shape[1] % (cols * LANES) == 0
         and n <= 16
+        and n & (n - 1) == 0
     )
 
 

time: 25.6 us -> 23.1 us (0.902)
  Pallas kernels: 24.1 us -> 21.6 us
    pallas_call x1, Pallas kernels: 24.1 us -> 21.6 us  [fused(): pl.pallas_call(functools.partial(score_kernel, n, cols, docs), name='scor...]
where the time goes in v2:
time: 23.1 us; the launch traced here: 22.9 us
  Pallas kernels  21.6 us (94%)
  local copies, waits for them, and re-layouts  1.3 us (6%)
    pallas_call x1, Pallas kernels, fused(): pl.pallas_call(functools.partial(score_kernel, n, cols, docs), name='scor...  21.6 us
    unnamed x1, local copies, waits for them, and re-layouts  1.3 us

profile of v2, /device:TPU:0, one launch (start us, length us, event | category | flops | bytes accessed | tf_op | source)
XLA Modules:
  0.0 22.9 jit_solution(2040832904733706920)
XLA Ops:
  0.0 21.6 %scores.1 = f32[12,64]{1,0:T(8,128)} custom-call(bf16[128,2048]{1,0:T(8,128)(2,1)} %act.1, bf16[128,7168]{1,0:T(8,128)(2,1)} %grad.1, s32[1,128]{1,0:T(1,128)} %bitcast.5, bf16[64,2048]{1,0:T(8,128)(2,1)} %bitcast.4, bf16[64,7168]{1,0:T(8,128)(2,1)} %bitcast.3, f32[2048,512]{1,0:T(8,128)} %inv.1, bf16[64,4096]{1,0:T(8,128)(2,1)} %store.1), custom_call_target="tpu_custom_call" | custom-call | tf_op jit(solution)/shard_map/scores/pallas_call | solution.py:257
  21.6 1.3 %copy.9 = f32[12,64]{1,0:T(8,128)} copy(f32[12,64]{1,0:T(8,128)} %scores.1) | data formatting | bytes 6144

commit v3 on v2

--- a/solution.py
+++ b/solution.py
@@ -71,10 +71,6 @@
     return order
 
 
-def q_order(n):
-    return sums_order(n) + [0]
-
-
 NT = (((1,), (1,)), ((), ()))
 
 
@@ -122,10 +118,10 @@
     barrier = pltpu.get_barrier_semaphore()
     ctx_peers = {r: {"ctx": jnp.bitwise_xor(me, r)} for r in sums_order(n)}
     peers = {}
-    for r in q_order(n):
+    for r in range(n):
         for d in range(cols):
             if r or d:
-                peers[cols * r + d] = {"ctx": jnp.bitwise_xor(me, r), "col": jnp.bitwise_xor(core, d)}
+                peers[cols * r + d] = {"ctx": lax.rem(me + r, n), "col": jnp.bitwise_xor(core, d)}
     for peer in peers.values():
         pl.semaphore_signal(barrier, inc=1, device_id=peer, device_id_type=MESH)
 

time: 23.1 us -> 22.7 us (0.983)
  Pallas kernels: 21.6 us -> 21.2 us
    pallas_call x1, Pallas kernels: 21.6 us -> 21.2 us  [fused(): pl.pallas_call(functools.partial(score_kernel, n, cols, docs), name='scor...]
where the time goes in v3:
time: 22.7 us; the launch traced here: 22.6 us
  Pallas kernels  21.2 us (93%)
  local copies, waits for them, and re-layouts  1.3 us (6%)
    pallas_call x1, Pallas kernels, fused(): pl.pallas_call(functools.partial(score_kernel, n, cols, docs), name='scor...  21.2 us
    unnamed x1, local copies, waits for them, and re-layouts  1.3 us

profile of v3, /device:TPU:0, one launch (start us, length us, event | category | flops | bytes accessed | tf_op | source)
XLA Modules:
  0.0 22.6 jit_solution(1774838758684189736)
XLA Ops:
  0.0 21.2 %scores.1 = f32[12,64]{1,0:T(8,128)} custom-call(bf16[128,2048]{1,0:T(8,128)(2,1)} %act.1, bf16[128,7168]{1,0:T(8,128)(2,1)} %grad.1, s32[1,128]{1,0:T(1,128)} %bitcast.5, bf16[64,2048]{1,0:T(8,128)(2,1)} %bitcast.4, bf16[64,7168]{1,0:T(8,128)(2,1)} %bitcast.3, f32[2048,512]{1,0:T(8,128)} %inv.1, bf16[64,4096]{1,0:T(8,128)(2,1)} %store.1), custom_call_target="tpu_custom_call" | custom-call | tf_op jit(solution)/shard_map/scores/pallas_call | solution.py:253
  21.3 1.3 %copy.9 = f32[12,64]{1,0:T(8,128)} copy(f32[12,64]{1,0:T(8,128)} %scores.1) | data formatting | bytes 6144
